TPU v7x, 32 devices: a whole 2x2x4 slice. The times are simulated.
32 devices in a mesh: heads: 4 (over y, core), seq: 8 (over z, x).
Axes of the slice: x: 2, y: 2, z: 4, core: 2. Of those that a mesh axis runs over, the one named last changes fastest.
Arguments:
- queries: bfloat16 [1024, 64, 576], P('seq', 'heads'), may hold values from -6 to 6
- latents: bfloat16 [8, 128, 576], P('seq', 'heads'), may hold values from -6 to 6
- grad_out: bfloat16 [1024, 64, 512], P('seq', 'heads'), may hold values from -6 to 6
- selected: int32 [8, 4], P('seq'), may hold values from 0 to 7, as said below
Outputs:
- output: bfloat16 [1024, 64, 512], P('seq', 'heads')
- grad_query: bfloat16 [1024, 64, 576], P('seq', 'heads')
- latent_grad: float32 [8, 128, 576], P('seq', 'heads')
Inputs may be any that keep to these rules, and one draw needn't show every extreme that they name: `selected`: row i lists 4 different blocks, none of them held on the same index of seq as block i (blocks i and j share it when i // 1 equals j // 1); how often a block is chosen varies widely between blocks.
All inputs are finite; a program needn't handle non-finite values.
Results may differ from a plain program's by a relative error of at most 0.012.
Values may be sent and summed in bfloat16 or wider, within the bound.
A program may use at most 64 MiB of HBM per device.

v0:
```python
import jax
import jax.numpy as jnp
from jax import lax
from jax.sharding import PartitionSpec as P


def shards(queries, latents, grad_out, selected):
    block_count, row_share, key_width = latents.shape
    token_total, head_count, _ = queries.shape
    value_width = grad_out.shape[2]
    key_blocks = selected.shape[1] + 1
    block_size = token_total // block_count
    score_scale = key_width ** (-0.5)
    slices = lax.all_gather(latents, "seq", axis=0, tiled=True)
    list_blocks = slices.shape[0]
    own_blocks = lax.axis_index("seq") * block_count + jnp.arange(block_count, dtype=jnp.int32)
    block_ids = jnp.concatenate([own_blocks[:, None], selected], axis=1).reshape(-1)
    picked = jnp.take(slices, block_ids, axis=0)
    key_row_tiles = lax.all_gather(picked, "heads", axis=1, tiled=True)
    key_row_tiles = key_row_tiles.reshape(block_count, key_blocks * block_size, key_width)
    value_rows = key_row_tiles[:, :, :value_width]
    query_row_tiles = queries.reshape(block_count, block_size, head_count, key_width)
    grad_rows = grad_out.reshape(block_count, block_size, head_count, value_width)
    scores = (
        jnp.einsum(
            "gonv,gmv->gnom", query_row_tiles, key_row_tiles, preferred_element_type=jnp.float32
        )
        * score_scale
    )
    prob_full = jax.nn.softmax(scores, axis=-1)
    prob_half = prob_full.astype(jnp.bfloat16)
    output = jnp.einsum(
        "bhtk,bkl->bthl", prob_half, value_rows, preferred_element_type=jnp.float32
    ).astype(jnp.bfloat16)
    row_delta = jnp.sum(grad_rows.astype(jnp.float32) * output.astype(jnp.float32), axis=-1)
    grad_prob = jnp.einsum(
        "bthl,bkl->bhtk", grad_rows, value_rows, preferred_element_type=jnp.float32
    )
    score_gradient = (
        prob_full * (grad_prob - jnp.transpose(row_delta, (0, 2, 1))[..., None]) * score_scale
    ).astype(jnp.bfloat16)
    grad_query = jnp.einsum(
        "mfgv,mvq->mgfq", score_gradient, key_row_tiles, preferred_element_type=jnp.float32
    ).astype(jnp.bfloat16)
    key_gradient = jnp.einsum(
        "jxnq,jnxa->jqa", score_gradient, query_row_tiles, preferred_element_type=jnp.float32
    )
    grad_value = jnp.einsum(
        "bhtk,bthl->bkl", prob_half, grad_rows, preferred_element_type=jnp.float32
    )
    key_gradient = jnp.concatenate(
        [key_gradient[:, :, :value_width] + grad_value, key_gradient[:, :, value_width:]], axis=-1
    )
    contrib = key_gradient.reshape(block_count * key_blocks, block_size, key_width)
    head_total = lax.psum(contrib, "heads")
    own_share = lax.dynamic_slice_in_dim(
        head_total, lax.axis_index("heads") * row_share, row_share, 1
    )
    one_hot = (jnp.arange(list_blocks, dtype=jnp.int32)[:, None] == block_ids[None, :]).astype(
        jnp.float32
    )
    dense_grad = jnp.dot(
        one_hot,
        own_share.reshape(block_count * key_blocks, row_share * key_width),
        precision=lax.Precision.HIGHEST,
        preferred_element_type=jnp.float32,
    )
    dense_grad = dense_grad.reshape(list_blocks, row_share, key_width)
    holders = list_blocks // block_count
    bundles = dense_grad.reshape(1, holders * block_count, row_share, key_width)
    arrived = lax.all_to_all(bundles, "seq", split_axis=1, concat_axis=0, tiled=True)
    latent_grad = jnp.sum(arrived, axis=0)
    return (
        output.reshape(token_total, head_count, value_width),
        grad_query.reshape(token_total, head_count, key_width),
        latent_grad,
    )


def solution(mesh):
    in_specs = (
        P("seq", "heads", None),
        P("seq", "heads", None),
        P("seq", "heads", None),
        P("seq", None),
    )
    out_specs = (P("seq", "heads", None), P("seq", "heads", None), P("seq", "heads", None))
    return jax.shard_map(shards, mesh=mesh, in_specs=in_specs, out_specs=out_specs, check_vma=False)
```

profile of v0, /device:TPU:0, one launch (start us, length us, event | category | flops | bytes accessed | tf_op | source)
XLA Modules:
  0.0 150.2 jit_solution(12962128840217296627)
XLA Ops:
  7.2 0.0 copy-start
  7.2 0.0 all-reduce.2.cloned.1.call-start
  7.2 0.9 compare_and_fusion
  8.1 32.9 %all_gather.6 = bf16[8,32,576]{2,1,0:T(8,128)(2,1)S(1)} all-gather(bf16[1,32,576]{2,1,0:T(8,128)(2,1)} %param.5), channel_id=1, replica_groups=mesh['heads'=4,'seq'=8] {'seq'}, dimensions={0}, use_global_device_ids=true | all-gather | bytes 331776 | tf_op jit(solution)/shard_map/all_gather | solution.py:14
  41.0 0.6 gather_fusion
  41.6 0.1 broadcast_select_fusion
  41.7 8.8 %all_gather.7 = bf16[5,128,576]{2,1,0:T(8,128)(2,1)S(1)} all-gather(bf16[5,32,576]{2,1,0:T(8,128)(2,1)S(1)} %broadcast_select_fusion), channel_id=1, replica_groups=mesh['heads'=4,'seq'=8] {'heads'}, dimensions={1}, use_global_device_ids=true | all-gather | bytes 921600 | tf_op jit(solution)/shard_map/all_gather | solution.py:19
  50.5 0.0 copy-start.2
  50.5 4.8 %copy.37 = bf16[128,16,512]{0,2,1:T(8,128)(2,1)} copy(bf16[128,16,512]{2,1,0:T(8,128)(2,1)} %param.6) | data formatting | bytes 4194304 | tf_op args[2]
  55.3 0.0 copy-done
  55.3 2.2 %bitcast_reduce_fusion = (f32[16,128]{1,0:T(8,128)S(1)}, f32[640,128,16]{1,0,2:T(8,128)S(1)}) fusion(bf16[640,576,1]{1,0,2:T(8,128)(2,1)S(1)} %bitcast.124, bf16[128,16,576]{0,2,1:T(8,128)(2,1)S(1)} %copy-done), kind=kOutput, calls=%fused_computation.6 | convolution fusion | flops 1512568832 | bytes 8347648 | tf_op jit(solution)/shard_map/gonv,gmv->gnom/dot_general | solution.py:25
  57.5 0.0 copy-start.1
  57.5 0.9 fusion.5
  58.4 0.7 copy-done.1
  59.1 3.5 %fusion.6 = (f32[128,16]{0,1:T(8,128)S(1)}, bf16[512,16,128]{2,0,1:T(8,128)(2,1)}) fusion(bf16[128,16,512]{0,2,1:T(8,128)(2,1)S(1)} %copy-done.1, f32[16,128]{1,0:T(8,128)S(1)} %fusion.5, f32[16,128]{1,0:T(8,128)S(1)} %get-tuple-element.14, f32[640,128,16]{1,0,2:T(8,128)S(1)} %get-tuple-element.15, bf16[1,640,576]{2,1,0:T(8,128)(2,1)S(1)} %bitcast.125), kind=kOutput, calls=%fused_computation.11 | convolution fusion | flops 1352660992 | bytes 10117120 | tf_op jit(solution)/shard_map/bhtk,bkl->bthl/dot_general | solution.py:32
  62.6 0.0 copy-done.2
  62.6 2.0 %fusion.7 = bf16[16,128,640]{1,2,0:T(8,128)(2,1)S(1)} fusion(f32[16,128]{1,0:T(8,128)S(1)} %bitcast.130, f32[16,128]{1,0:T(8,128)S(1)} %fusion.5, f32[16,128]{1,0:T(8,128)S(1)} %get-tuple-element.14, f32[640,128,16]{1,0,2:T(8,128)S(1)} %get-tuple-element.15, bf16[128,16,512]{0,2,1:T(8,128)(2,1)S(1)} %copy-done.1, bf16[1,640,576]{2,1,0:T(8,128)(2,1)S(1)} %bitcast.126), kind=kOutput, calls=%fused_computation.12 | convolution fusion | flops 1351352320 | bytes 10641408 | tf_op jit(solution)/shard_map/bthl,bkl->bhtk/dot_general | solution.py:36
  64.6 0.0 copy-start.3
  64.6 2.0 %convolution_bitcast_fusion = f32[1,640,576]{1,2,0:T(8,128)S(1)} fusion(bf16[16,128,640]{1,2,0:T(8,128)(2,1)S(1)} %fusion.7, bf16[128,16,576]{0,2,1:T(8,128)(2,1)S(1)} %copy-done), kind=kOutput, calls=%fused_computation.21 | convolution fusion | flops 1509949440 | bytes 6455296 | tf_op jit(solution)/shard_map/jxnq,jnxa->jqa/dot_general | solution.py:45
  66.6 0.0 copy-done.3
  66.6 1.9 %fusion.19 = f32[1,640,512]{1,2,0:T(8,128)S(1)} fusion(bf16[128,16,512]{0,2,1:T(8,128)(2,1)S(1)} %copy-done.1, f32[1,640,576]{1,2,0:T(8,128)S(1)} %convolution_bitcast_fusion, f32[16,128]{1,0:T(8,128)S(1)} %fusion.5, f32[16,128]{1,0:T(8,128)S(1)} %get-tuple-element.14, f32[640,128,16]{1,0,2:T(8,128)S(1)} %get-tuple-element.15), kind=kOutput, calls=%fused_computation.23 | convolution fusion | flops 1347747840 | bytes 9977856 | tf_op jit(solution)/shard_map/bhtk,bthl->bkl/dot_general | solution.py:48
  68.6 1.2 pad_maximum_fusion
  69.8 3.0 %copy.43 = f32[1,640,576]{2,1,0:T(8,128)} copy(f32[1,640,576]{1,2,0:T(8,128)} %pad_maximum_fusion) | data formatting | bytes 2949120 | tf_op jit(solution)/shard_map/concatenate | solution.py:51
  72.8 0.0 all-reduce.2.cloned.1.call-update
  72.8 44.1 %all-reduce.2.cloned.1.call-done = f32[5,128,576]{2,1,0:T(8,128)} async-done(((f32[5,128,576]{2,1,0:T(8,128)}), f32[5,128,576]{2,1,0:T(8,128)}) %all-reduce.2.cloned.1.call-update) | async-done | bytes 1474576 | tf_op jit(solution)/shard_map/psum | solution.py:55
  117.0 1.0 constant_dynamic-slice_fusion
  118.0 0.2 reshape.186
  118.2 0.2 dot_general.43
  118.4 0.7 convolution_bitcast_fusion.1
  119.1 1.0 copy.45
  120.0 5.5 %all-to-all-start = ((f32[1,8,32,576]{3,2,0,1:T(8,128)}), f32[1,8,32,576]{3,2,0,1:T(8,128)S(1)}, u32[]{:S(2)}, u32[]{:S(2)}) async-start(f32[1,8,32,576]{3,2,0,1:T(8,128)} %copy.45), calls=%async_computation | async-start | bytes 1310720 | tf_op jit(solution)/shard_map/all_to_all | solution.py:71
  125.5 4.5 %copy.46 = bf16[128,16,512]{2,1,0:T(8,128)(2,1)} copy(bf16[128,16,512]{0,2,1:T(8,128)(2,1)} %bitcast.123) | data formatting | bytes 4194304
  130.1 5.4 %convert_bitcast_fusion = bf16[128,16,576]{0,2,1:T(8,128)(2,1)} fusion(bf16[640,576,1]{1,0,2:T(8,128)(2,1)} %bitcast.127, bf16[16,128,640]{1,2,0:T(8,128)(2,1)} %copy-done.3), kind=kOutput, calls=%fused_computation.18 | convolution fusion | flops 1511129088 | bytes 5718016 | tf_op jit(solution)/shard_map/mfgv,mvq->mgfq/dot_general | solution.py:42
  135.5 7.2 %all-to-all-done = f32[1,8,32,576]{3,2,0,1:T(8,128)S(1)} async-done(((f32[1,8,32,576]{3,2,0,1:T(8,128)}), f32[1,8,32,576]{3,2,0,1:T(8,128)S(1)}, u32[]{:S(2)}, u32[]{:S(2)}) %all-to-all-start) | async-done | bytes 589856 | tf_op jit(solution)/shard_map/all_to_all | solution.py:71
  142.7 0.7 reduce_sum.34
  (3 shorter events, 0.0 us)
Async XLA Ops:
  7.2 48.1 %copy-start = (bf16[128,16,576]{0,2,1:T(8,128)(2,1)S(1)}, bf16[128,16,576]{0,2,1:T(8,128)(2,1)}, u32[]{:S(2)}) copy-start(bf16[128,16,576]{0,2,1:T(8,128)(2,1)} %param.4) | copy-start | bytes 7077892
  7.2 109.8 %all-reduce.2.cloned.1.call-start = ((), (), s32[]{:S(2)}) async-start(), calls=%async_computation.1 | async-start | bytes 3276800 | tf_op jit(solution)/shard_map/psum | solution.py:55
  50.5 12.1 %copy-start.2 = (bf16[5,128,576]{2,1,0:T(8,128)(2,1)}, bf16[5,128,576]{2,1,0:T(8,128)(2,1)S(1)}, u32[]{:S(2)}) copy-start(bf16[5,128,576]{2,1,0:T(8,128)(2,1)S(1)} %all_gather.7) | copy-start | bytes 2211844
  57.5 1.6 %copy-start.1 = (bf16[128,16,512]{0,2,1:T(8,128)(2,1)S(1)}, bf16[128,16,512]{0,2,1:T(8,128)(2,1)}, u32[]{:S(2)}) copy-start(bf16[128,16,512]{0,2,1:T(8,128)(2,1)} %copy.37) | copy-start | bytes 6291460
  64.6 2.0 %copy-start.3 = (bf16[16,128,640]{1,2,0:T(8,128)(2,1)}, bf16[16,128,640]{1,2,0:T(8,128)(2,1)S(1)}, u32[]{:S(2)}) copy-start(bf16[16,128,640]{1,2,0:T(8,128)(2,1)S(1)} %fusion.7) | copy-start | bytes 7864324
  120.0 22.7 %all-to-all-start = ((f32[1,8,32,576]{3,2,0,1:T(8,128)}), f32[1,8,32,576]{3,2,0,1:T(8,128)S(1)}, u32[]{:S(2)}, u32[]{:S(2)}) async-start(f32[1,8,32,576]{3,2,0,1:T(8,128)} %copy.45), calls=%async_computation | async-start | bytes 1310720 | tf_op jit(solution)/shard_map/all_to_all | solution.py:71
Sparse Core Ops, SparseCore 0:
  73.0 43.9 all-reduce.1
where the time goes:
time: 151 us; the launch traced here: 150 us
  waiting for transfers between devices  51.3 us (34%)
  blocking collectives  41.7 us (28%)
  matrix products  17.7 us (12%)
  local copies, waits for them, and re-layouts  16.1 us (11%)
  between operations  14.1 us (9%)
  starting transfers between devices  5.55 us (4%)
  other arithmetic  3.74 us (2%)
    psum x1, waiting for transfers between devices, shards(): head_total = lax.psum(contrib, 'heads')  44.1 us
    all_gather x1, blocking collectives, shards(): slices = lax.all_gather(latents, 'seq', axis=0, tiled=True)  32.9 us
    unnamed x10, local copies, waits for them, and re-layouts  10 us
    all_gather x1, blocking collectives, shards(): key_row_tiles = lax.all_gather(picked, 'heads', axis=1, tiled=True)  8.8 us
    all_to_all x1, waiting for transfers between devices, shards(): lax.all_to_all(bundles, 'seq', split_axis=1, concat_axis=0, tiled=True)  7.21 us
    all_to_all x1, starting transfers between devices, shards(): lax.all_to_all(bundles, 'seq', split_axis=1, concat_axis=0, tiled=True)  5.51 us
    dot_general x1, matrix products, shards(): jnp.einsum('mfgv,mvq->mgfq', score_gradient, key_row_tiles, preferred_ele...  5.43 us
    dot_general x1, matrix products, shards(): jnp.einsum('bhtk,bkl->bthl', prob_half, value_rows, preferred_element_typ...  3.47 us
  transfers between devices with their start and end apart: 2, of which 2 were waited for; matrix products, arithmetic and copies ran while one was open for 7% of the time, Pallas kernels for 0%

commit v1 on v0

--- a/solution.py
+++ b/solution.py
@@ -52,7 +52,8 @@
         [key_gradient[:, :, :value_width] + grad_value, key_gradient[:, :, value_width:]], axis=-1
     )
     contrib = key_gradient.reshape(block_count * key_blocks, block_size, key_width)
-    head_total = lax.psum(contrib, "heads")
+    parts = lax.all_gather(contrib, "heads", axis=0, tiled=False)
+    head_total = parts.sum(axis=0)
     own_share = lax.dynamic_slice_in_dim(
         head_total, lax.axis_index("heads") * row_share, row_share, 1
     )

time: 151 us -> 163 us (1.079)
  local copies, waits for them, and re-layouts: 16.1 us -> 23 us
  other arithmetic: 3.74 us -> 8.02 us
    all_gather x0 -> x1, waiting for transfers between devices: none -> 44.3 us  [shards(): parts = lax.all_gather(contrib, 'heads', axis=0, tiled=False)]
    psum x1 -> x0, waiting for transfers between devices: 44.1 us -> none  [shards(): head_total = lax.psum(contrib, 'heads')]
    reduce_sum x0 -> x1, other arithmetic: none -> 4.26 us  [shards(): head_total = parts.sum(axis=0)]
    dynamic_slice x1 -> x2, local copies, waits for them, and re-layouts: 1.03 us -> 4.79 us  [shards(): lax.dynamic_slice_in_dim(head_total, lax.axis_index('heads') * row_share,...]
    another operation x0 -> x1, local copies, waits for them, and re-layouts: none -> 3.11 us  [shards(): parts = lax.all_gather(contrib, 'heads', axis=0, tiled=False)]
  transfers between devices with their start and end apart: 2 -> 2, of which waited for: 2 -> 2; matrix products, arithmetic and copies ran while one was open for 7% -> 6% of each run, Pallas kernels for 0% -> 0%
where the time goes in v1:
time: 163 us; the launch traced here: 162 us
  waiting for transfers between devices  52.1 us (32%)
  blocking collectives  41.7 us (26%)
  local copies, waits for them, and re-layouts  23 us (14%)
  matrix products  17.9 us (11%)
  between operations  14.1 us (9%)
  other arithmetic  8.02 us (5%)
  starting transfers between devices  5.55 us (3%)
    all_gather x1, waiting for transfers between devices, shards(): parts = lax.all_gather(contrib, 'heads', axis=0, tiled=False)  44.3 us
    all_gather x1, blocking collectives, shards(): slices = lax.all_gather(latents, 'seq', axis=0, tiled=True)  32.9 us
    unnamed x10, local copies, waits for them, and re-layouts  10 us
    all_gather x1, blocking collectives, shards(): key_row_tiles = lax.all_gather(picked, 'heads', axis=1, tiled=True)  8.8 us
    all_to_all x1, waiting for transfers between devices, shards(): lax.all_to_all(bundles, 'seq', split_axis=1, concat_axis=0, tiled=True)  7.77 us
    all_to_all x1, starting transfers between devices, shards(): lax.all_to_all(bundles, 'seq', split_axis=1, concat_axis=0, tiled=True)  5.51 us
    dot_general x1, matrix products, shards(): jnp.einsum('mfgv,mvq->mgfq', score_gradient, key_row_tiles, preferred_ele...  5.43 us
    dynamic_slice x2, local copies, waits for them, and re-layouts, shards(): lax.dynamic_slice_in_dim(head_total, lax.axis_index('heads') * row_share,...  4.79 us
  transfers between devices with their start and end apart: 2, of which 2 were waited for; matrix products, arithmetic and copies ran while one was open for 6% of the time, Pallas kernels for 0%

profile of v1, /device:TPU:0, one launch (start us, length us, event | category | flops | bytes accessed | tf_op | source)
XLA Modules:
  0.0 162.4 jit_solution(16008847229562464408)
XLA Ops:
  7.2 0.0 copy-start
  7.2 0.0 all-gather.2.cloned.1.call-start
  7.2 0.9 compare_and_fusion
  8.1 32.9 %all_gather.9 = bf16[8,32,576]{2,1,0:T(8,128)(2,1)S(1)} all-gather(bf16[1,32,576]{2,1,0:T(8,128)(2,1)} %param.5), channel_id=1, replica_groups=mesh['heads'=4,'seq'=8] {'seq'}, dimensions={0}, use_global_device_ids=true | all-gather | bytes 331776 | tf_op jit(solution)/shard_map/all_gather | solution.py:14
  41.0 0.6 gather_fusion
  41.6 0.1 broadcast_select_fusion
  41.7 8.8 %all_gather.10 = bf16[5,128,576]{2,1,0:T(8,128)(2,1)S(1)} all-gather(bf16[5,32,576]{2,1,0:T(8,128)(2,1)S(1)} %broadcast_select_fusion), channel_id=1, replica_groups=mesh['heads'=4,'seq'=8] {'heads'}, dimensions={1}, use_global_device_ids=true | all-gather | bytes 921600 | tf_op jit(solution)/shard_map/all_gather | solution.py:19
  50.5 0.0 copy-start.2
  50.5 4.8 %copy.69 = bf16[128,16,512]{0,2,1:T(8,128)(2,1)} copy(bf16[128,16,512]{2,1,0:T(8,128)(2,1)} %param.6) | data formatting | bytes 4194304 | tf_op args[2]
  55.3 0.0 copy-done
  55.3 2.2 %bitcast_reduce_fusion = (f32[16,128]{1,0:T(8,128)S(1)}, f32[640,128,16]{1,0,2:T(8,128)S(1)}) fusion(bf16[640,576,1]{1,0,2:T(8,128)(2,1)S(1)} %bitcast.124, bf16[128,16,576]{0,2,1:T(8,128)(2,1)S(1)} %copy-done), kind=kOutput, calls=%fused_computation.6 | convolution fusion | flops 1512568832 | bytes 8347648 | tf_op jit(solution)/shard_map/gonv,gmv->gnom/dot_general | solution.py:25
  57.5 0.0 copy-start.1
  57.5 0.9 fusion.5
  58.4 0.7 copy-done.1
  59.1 3.5 %fusion.6 = (f32[128,16]{0,1:T(8,128)S(1)}, bf16[512,16,128]{2,0,1:T(8,128)(2,1)}) fusion(bf16[128,16,512]{0,2,1:T(8,128)(2,1)S(1)} %copy-done.1, f32[16,128]{1,0:T(8,128)S(1)} %fusion.5, f32[16,128]{1,0:T(8,128)S(1)} %get-tuple-element.20, f32[640,128,16]{1,0,2:T(8,128)S(1)} %get-tuple-element.21, bf16[1,640,576]{2,1,0:T(8,128)(2,1)S(1)} %bitcast.125), kind=kOutput, calls=%fused_computation.11 | convolution fusion | flops 1352660992 | bytes 10117120 | tf_op jit(solution)/shard_map/bhtk,bkl->bthl/dot_general | solution.py:32
  62.6 0.0 copy-done.2
  62.6 2.2 %fusion.7 = bf16[16,128,640]{1,2,0:T(8,128)(2,1)S(1)} fusion(f32[16,128]{1,0:T(8,128)S(1)} %bitcast.130, f32[16,128]{1,0:T(8,128)S(1)} %fusion.5, f32[16,128]{1,0:T(8,128)S(1)} %get-tuple-element.20, f32[640,128,16]{1,0,2:T(8,128)S(1)} %get-tuple-element.21, bf16[128,16,512]{0,2,1:T(8,128)(2,1)S(1)} %copy-done.1, bf16[1,640,576]{2,1,0:T(8,128)(2,1)S(1)} %bitcast.126), kind=kOutput, calls=%fused_computation.12 | convolution fusion | flops 1351352320 | bytes 10641408 | tf_op jit(solution)/shard_map/bthl,bkl->bhtk/dot_general | solution.py:36
  64.8 0.0 copy-start.3
  64.8 2.0 %convolution_bitcast_fusion = f32[1,640,576]{1,2,0:T(8,128)S(1)} fusion(bf16[16,128,640]{1,2,0:T(8,128)(2,1)S(1)} %fusion.7, bf16[128,16,576]{0,2,1:T(8,128)(2,1)S(1)} %copy-done), kind=kOutput, calls=%fused_computation.21 | convolution fusion | flops 1509949440 | bytes 6455296 | tf_op jit(solution)/shard_map/jxnq,jnxa->jqa/dot_general | solution.py:45
  66.8 0.0 copy-done.3
  66.8 1.9 %fusion.19 = f32[1,640,512]{1,2,0:T(8,128)S(1)} fusion(bf16[128,16,512]{0,2,1:T(8,128)(2,1)S(1)} %copy-done.1, f32[1,640,576]{1,2,0:T(8,128)S(1)} %convolution_bitcast_fusion, f32[16,128]{1,0:T(8,128)S(1)} %fusion.5, f32[16,128]{1,0:T(8,128)S(1)} %get-tuple-element.20, f32[640,128,16]{1,0,2:T(8,128)S(1)} %get-tuple-element.21), kind=kOutput, calls=%fused_computation.23 | convolution fusion | flops 1347747840 | bytes 9977856 | tf_op jit(solution)/shard_map/bhtk,bthl->bkl/dot_general | solution.py:48
  68.7 1.2 pad_maximum_fusion
  70.0 3.0 %copy.75 = f32[1,640,576]{2,1,0:T(8,128)} copy(f32[1,640,576]{1,2,0:T(8,128)} %pad_maximum_fusion) | data formatting | bytes 2949120 | tf_op jit(solution)/shard_map/concatenate | solution.py:51
  73.0 3.1 %copy.76 = f32[1,5,128,576]{2,3,1,0:T(8,128)} copy(f32[1,5,128,576]{3,2,1,0:T(8,128)} %bitcast.121) | data formatting | bytes 2949120 | tf_op jit(solution)/shard_map/all_gather;reshape | solution.py:55
  76.1 0.0 all-gather.2.cloned.1.call-update
  76.1 44.3 %all-gather.2.cloned.1.call-done = f32[4,5,128,576]{2,3,1,0:T(8,128)} async-done(((f32[1,5,128,576]{2,3,1,0:T(8,128)}), f32[4,5,128,576]{2,3,1,0:T(8,128)}) %all-gather.2.cloned.1.call-update) | async-done | bytes 5898256 | tf_op jit(solution)/shard_map/all_gather | solution.py:55
  120.5 4.3 %reduce_sum.43 = f32[5,128,576]{1,2,0:T(8,128)} reduce(f32[4,5,128,576]{2,3,1,0:T(8,128)} %all-gather.2.cloned.1.call-done, f32[]{:T(128)} %constant.32.clone.1), dimensions={0}, to_apply=%region_3.4 | reduce | flops 1105920 | bytes 7372804 | tf_op jit(solution)/shard_map/reduce_sum | solution.py:56
  124.7 3.0 %constant_dynamic-slice_fusion = f32[5,32,576]{1,2,0:T(8,128)} fusion(f32[5,128,576]{1,2,0:T(8,128)} %reduce_sum.43, s32[]{:T(128)S(6)} %select_n.26), kind=kLoop, calls=%fused_computation.37 | loop fusion | bytes 737284 | tf_op jit(solution)/shard_map/dynamic_slice | solution.py:57
  127.7 1.8 %copy.77 = f32[5,32,576]{2,1,0:T(8,128)S(1)} copy(f32[5,32,576]{1,2,0:T(8,128)} %constant_dynamic-slice_fusion) | data formatting | bytes 737280 | tf_op jit(solution)/shard_map/dynamic_slice | solution.py:57
  129.5 0.2 reshape.182
  129.8 0.2 dot_general.43
  130.0 0.7 convolution_bitcast_fusion.1
  130.6 1.0 copy.79
  131.6 5.5 %all-to-all-start = ((f32[1,8,32,576]{3,2,0,1:T(8,128)}), f32[1,8,32,576]{3,2,0,1:T(8,128)S(1)}, u32[]{:S(2)}, u32[]{:S(2)}) async-start(f32[1,8,32,576]{3,2,0,1:T(8,128)} %copy.79), calls=%async_computation | async-start | bytes 1310720 | tf_op jit(solution)/shard_map/all_to_all | solution.py:72
  137.1 4.5 %copy.80 = bf16[128,16,512]{2,1,0:T(8,128)(2,1)} copy(bf16[128,16,512]{0,2,1:T(8,128)(2,1)} %bitcast.123) | data formatting | bytes 4194304
  141.6 5.4 %convert_bitcast_fusion = bf16[128,16,576]{0,2,1:T(8,128)(2,1)} fusion(bf16[640,576,1]{1,0,2:T(8,128)(2,1)} %bitcast.127, bf16[16,128,640]{1,2,0:T(8,128)(2,1)} %copy-done.3), kind=kOutput, calls=%fused_computation.18 | convolution fusion | flops 1511129088 | bytes 5718016 | tf_op jit(solution)/shard_map/mfgv,mvq->mgfq/dot_general | solution.py:42
  147.1 7.8 %all-to-all-done = f32[1,8,32,576]{3,2,0,1:T(8,128)S(1)} async-done(((f32[1,8,32,576]{3,2,0,1:T(8,128)}), f32[1,8,32,576]{3,2,0,1:T(8,128)S(1)}, u32[]{:S(2)}, u32[]{:S(2)}) %all-to-all-start) | async-done | bytes 589856 | tf_op jit(solution)/shard_map/all_to_all | solution.py:72
  154.8 0.7 reduce_sum.44
  (3 shorter events, 0.0 us)
Async XLA Ops:
  7.2 48.1 %copy-start = (bf16[128,16,576]{0,2,1:T(8,128)(2,1)S(1)}, bf16[128,16,576]{0,2,1:T(8,128)(2,1)}, u32[]{:S(2)}) copy-start(bf16[128,16,576]{0,2,1:T(8,128)(2,1)} %param.4) | copy-start | bytes 7077892
  7.2 113.3 %all-gather.2.cloned.1.call-start = ((), (), s32[]{:S(2)}) async-start(), calls=%async_computation.1 | async-start | bytes 7372800 | tf_op jit(solution)/shard_map/all_gather | solution.py:55
  50.5 12.1 %copy-start.2 = (bf16[5,128,576]{2,1,0:T(8,128)(2,1)}, bf16[5,128,576]{2,1,0:T(8,128)(2,1)S(1)}, u32[]{:S(2)}) copy-start(bf16[5,128,576]{2,1,0:T(8,128)(2,1)S(1)} %all_gather.10) | copy-start | bytes 2211844
  57.5 1.6 copy-start.1
  64.8 2.0 %copy-start.3 = (bf16[16,128,640]{1,2,0:T(8,128)(2,1)}, bf16[16,128,640]{1,2,0:T(8,128)(2,1)S(1)}, u32[]{:S(2)}) copy-start(bf16[16,128,640]{1,2,0:T(8,128)(2,1)S(1)} %fusion.7) | copy-start | bytes 7864324
  131.6 23.2 %all-to-all-start = ((f32[1,8,32,576]{3,2,0,1:T(8,128)}), f32[1,8,32,576]{3,2,0,1:T(8,128)S(1)}, u32[]{:S(2)}, u32[]{:S(2)}) async-start(f32[1,8,32,576]{3,2,0,1:T(8,128)} %copy.79), calls=%async_computation | async-start | bytes 1310720 | tf_op jit(solution)/shard_map/all_to_all | solution.py:72
Sparse Core Ops, SparseCore 0:
  76.3 44.1 all-gather.1
